TPU v7x, 32 devices: a whole 2x2x4 slice. The times are simulated.
32 devices in a mesh: group: 8 (over z, x), fsdp: 4 (over y, core).
Axes of the slice: x: 2, y: 2, z: 4, core: 2. Of those that a mesh axis runs over, the one named last changes fastest.
Arguments:
- mol_qkv: bfloat16 [64, 128, 3, 4096], P('group', None, None, 'fsdp'), may hold values from -12 to 12
- pair_list: int32 [128, 3], replicated, may hold values from 0 to 7, as said below
- head_proj: bfloat16 [32, 128, 256], P('fsdp'), may hold values from -0.5 to 0.5
- head_out: float32 [32, 256], P('fsdp'), may hold values from -0.375 to 0.375
- labels: int32 [128], P('group'), may hold values 0 or 1
Outputs:
- mol_grad: bfloat16 [64, 128, 3, 4096], P('group', None, None, 'fsdp')
- pair_logits: float32 [128], P('group')
- mean_loss: float32 [], replicated
Inputs may be any that keep to these rules, and one draw needn't show every extreme that they name: `pair_list`: pair p belongs to owner p // 16; column 0 is the first molecule's index among the owner's 8 molecules, column 1 the group index that holds the second molecule, column 2 its index among that holder's 8 molecules; molecule m is held by group m // 8. `pair_list`: among one owner's pairs, at most 4 take their second molecule from any one holder, and those name at most 2 different molecules; every owner reaches both bounds.
All inputs are finite; a program needn't handle non-finite values. No bound on the sum of `labels` on one device may be relied on, other than what follows from the above.
Results may differ from a plain program's by a relative error of at most 0.0075.
Values may be sent and summed in bfloat16 or wider, within the bound.
A program may use at most 192 MiB of HBM per device.

v0:
```python
import jax
import jax.numpy as jnp
from jax import lax
from jax.sharding import PartitionSpec as P

loss_scale = 8192.0


def split_heads(rows_in, component, heads, head_dim):
    return rows_in[:, :, component].reshape(rows_in.shape[0], rows_in.shape[1], heads, head_dim)


def forward(query_rows, key_rows, value_rows, head_proj, head_out, inv_root, length):
    scores = (
        jnp.einsum("plhd,pmhd->phlm", query_rows, key_rows, preferred_element_type=jnp.float32)
        * inv_root
    )
    row_max = jnp.max(scores, axis=-1, keepdims=True)
    lifted = jnp.exp(scores - row_max)
    attn_weights = lifted / jnp.sum(lifted, axis=-1, keepdims=True)
    weights_bf = attn_weights.astype(jnp.bfloat16)
    context = jnp.einsum(
        "phlm,pmhd->plhd", weights_bf, value_rows, preferred_element_type=jnp.float32
    ).astype(jnp.bfloat16)
    hidden = jnp.einsum("plhd,hdr->plhr", context, head_proj, preferred_element_type=jnp.float32)
    partial_value = jnp.sum(jax.nn.silu(hidden) * head_out[None, None], axis=(1, 2, 3)) / length
    return (partial_value, (attn_weights, weights_bf, hidden))


def backward(
    query_rows, key_rows, value_rows, head_proj, head_out, saved, grad_out, inv_root, length
):
    attn_weights, weights_bf, hidden = saved
    sigmoid_h = jax.nn.sigmoid(hidden)
    silu_slope = sigmoid_h * (1.0 + hidden * (1.0 - sigmoid_h))
    dhidden = (grad_out[:, None, None, None] / length * head_out[None, None] * silu_slope).astype(
        jnp.bfloat16
    )
    dcontext = jnp.einsum(
        "plhr,hdr->plhd", dhidden, head_proj, preferred_element_type=jnp.float32
    ).astype(jnp.bfloat16)
    dvalues = jnp.einsum(
        "phlm,plhd->pmhd", weights_bf, dcontext, preferred_element_type=jnp.float32
    )
    dweights = jnp.einsum(
        "plhd,pmhd->phlm", dcontext, value_rows, preferred_element_type=jnp.float32
    )
    dscores = (
        attn_weights
        * (dweights - jnp.sum(dweights * attn_weights, axis=-1, keepdims=True))
        * inv_root
    ).astype(jnp.bfloat16)
    dqueries = jnp.einsum("phlm,pmhd->plhd", dscores, key_rows, preferred_element_type=jnp.float32)
    dkey_rows = jnp.einsum(
        "phlm,plhd->pmhd", dscores, query_rows, preferred_element_type=jnp.float32
    )
    return (dqueries, dkey_rows, dvalues)


def routing(blocks, mol_count, capacity, device):
    groups, per_owner, _ = blocks.shape
    holder = blocks[:, :, 1]
    member = blocks[:, :, 2]
    position = jnp.arange(per_owner, dtype=jnp.int32)
    mol_key = holder * mol_count + member
    matches = mol_key[:, :, None] == mol_key[:, None, :]
    earlier = matches & (position[None, None, :] < position[None, :, None])
    leading = jnp.logical_not(jnp.any(earlier, axis=2))
    leader = jnp.argmax(matches, axis=2)
    per_holder = (
        (holder[:, :, None] == jnp.arange(groups, dtype=jnp.int32)[None, None, :])
        & leading[:, :, None]
    ).astype(jnp.int32)
    rank_all = jnp.cumsum(per_holder, axis=1) - per_holder
    rank_in = jnp.take_along_axis(rank_all, holder[:, :, None], axis=2)[:, :, 0]
    slot_index = holder * capacity + rank_in
    return_slot = jnp.take_along_axis(slot_index, leader, axis=1)
    to_device = leading & (holder == device)
    picked = to_device[:, :, None] & (
        rank_in[:, :, None] == jnp.arange(capacity, dtype=jnp.int32)[None, None, :]
    )
    send_member = jnp.sum(picked.astype(jnp.int32) * member[:, :, None], axis=1)
    send_valid = jnp.any(picked, axis=1)
    return (return_slot, return_slot, send_member, send_valid)


def local(mol_qkv, pair_list, head_proj, head_out, labels):
    groups = lax.axis_size("group")
    device = lax.axis_index("group")
    mol_count, length, _, row_width = mol_qkv.shape
    heads_here, head_dim, inner_width = head_proj.shape
    total_pairs = pair_list.shape[0]
    per_owner = total_pairs // groups
    inv_root = head_dim ** (-0.5)
    blocks = pair_list.reshape(groups, per_owner, 3)
    capacity = per_owner // groups
    fetch_slot, return_slot, send_member, send_valid = routing(blocks, mol_count, capacity, device)
    slots_all = groups * capacity
    flat_member = send_member.reshape(slots_all)
    flat_valid = send_valid.reshape(slots_all)
    outgoing = jnp.take(mol_qkv, flat_member, axis=0)
    outgoing = jnp.where(flat_valid[:, None, None, None], outgoing, jnp.zeros_like(outgoing))
    incoming = lax.all_to_all(outgoing, "group", split_axis=0, concat_axis=0, tiled=True)
    my_pairs = lax.dynamic_index_in_dim(blocks, device, 0, keepdims=False)
    my_fetch = lax.dynamic_index_in_dim(fetch_slot, device, 0, keepdims=False)
    my_return = lax.dynamic_index_in_dim(return_slot, device, 0, keepdims=False)
    partner_rows = jnp.take(incoming, my_fetch, axis=0)
    own_rows = jnp.take(mol_qkv, my_pairs[:, 0], axis=0)
    qa, ka, va = [split_heads(own_rows, c, heads_here, head_dim) for c in range(3)]
    qb, kb, vb = [split_heads(partner_rows, c, heads_here, head_dim) for c in range(3)]
    part_ab, saved_ab = forward(qa, kb, vb, head_proj, head_out, inv_root, length)
    part_ba, saved_ba = forward(qb, ka, va, head_proj, head_out, inv_root, length)
    logits = lax.psum(part_ab + part_ba, "fsdp")
    targets = labels.astype(jnp.float32)
    loss_terms = jax.nn.softplus(logits) - targets * logits
    loss_sum = lax.psum(jnp.sum(loss_terms), "group")
    mean_loss = loss_sum / total_pairs
    grad_out = (jax.nn.sigmoid(logits) - targets) * loss_scale
    dq_a, dk_b, dv_b = backward(
        qa, kb, vb, head_proj, head_out, saved_ab, grad_out, inv_root, length
    )
    dq_b, dk_a, dv_a = backward(
        qb, ka, va, head_proj, head_out, saved_ba, grad_out, inv_root, length
    )
    grad_first = jnp.stack([dq_a, dk_a, dv_a], axis=2).reshape(per_owner, -1)
    grad_second = jnp.stack([dq_b, dk_b, dv_b], axis=2).reshape(per_owner, -1)
    own_pick = (my_pairs[:, 0][None, :] == jnp.arange(mol_count, dtype=jnp.int32)[:, None]).astype(
        jnp.float32
    )
    own_sum = jnp.dot(
        own_pick, grad_first, precision=lax.Precision.HIGHEST, preferred_element_type=jnp.float32
    )
    back_pick = (my_return[None, :] == jnp.arange(slots_all, dtype=jnp.int32)[:, None]).astype(
        jnp.float32
    )
    outgoing_grad = jnp.dot(
        back_pick, grad_second, precision=lax.Precision.HIGHEST, preferred_element_type=jnp.float32
    )
    outgoing_grad = outgoing_grad.astype(jnp.bfloat16).reshape(slots_all, length, 3, row_width)
    returned = lax.all_to_all(outgoing_grad, "group", split_axis=0, concat_axis=0, tiled=True)
    land_pick = (
        (flat_member[None, :] == jnp.arange(mol_count, dtype=jnp.int32)[:, None])
        & flat_valid[None, :]
    ).astype(jnp.bfloat16)
    partner_sum = jnp.dot(
        land_pick, returned.reshape(slots_all, -1), preferred_element_type=jnp.float32
    )
    mol_grad = (own_sum + partner_sum).astype(jnp.bfloat16).reshape(mol_qkv.shape)
    return (mol_grad, logits, mean_loss)


def solution(mesh):
    placed = (
        P("group", None, None, "fsdp"),
        P(),
        P("fsdp", None, None),
        P("fsdp", None),
        P("group"),
    )
    return jax.shard_map(
        local,
        mesh=mesh,
        in_specs=placed,
        out_specs=(P("group", None, None, "fsdp"), P("group"), P()),
        check_vma=False,
    )
```

profile of v0, /device:TPU:8, one launch (start us, length us, event | category | flops | bytes accessed | tf_op | source)
XLA Modules:
  0.0 1073.2 jit_solution(13335378748333062560)
XLA Ops:
  0.7 0.8 reshape.144
  1.5 0.3 fusion.127
  1.9 0.1 reshape.179
  2.0 0.1 copy.115
  2.1 0.1 reduce-window_subtract_fusion
  2.3 1.2 gather_fusion.1
  3.6 0.1 fusion.131
  3.8 0.2 select_reduce_fusion
  3.9 0.1 copy.116
  4.0 0.1 broadcast_in_dim.42
  4.1 0.1 copy.117
  4.2 0.1 reshape.147
  4.3 9.2 gather_fusion.3
  13.5 10.9 %select_select_fusion = bf16[16,128,3,1024]{3,1,2,0:T(8,128)(2,1)} fusion(bf16[16,128,3,1024]{3,1,2,0:T(8,128)(2,1)} %gather_fusion.3, pred[16]{0:T(512)(128)(4,1)S(1)} %get-tuple-element.46, pred[16]{0:T(512)(128)(4,1)S(1)} %broadcast_in_dim.42), kind=kLoop, calls=%fused_computation.43 | loop fusion | flops 12582912 | bytes 25165856 | tf_op jit(solution)/shard_map/jit(_where)/select_n | solution.py:102
  24.4 6.3 all-to-all-start
  30.6 1.0 compare_reduce_fusion
  31.6 0.1 reshape.185
  31.7 1.0 gather_fusion.2
  32.8 9.2 gather_fusion.4
  42.0 6.5 broadcast_select_fusion
  48.6 4.8 fusion.170
  53.4 6.4 copy.119
  59.8 6.4 copy.128
  66.2 6.4 copy.126
  72.6 0.5 compare_and_fusion.3
  73.1 228.0 %all-to-all-done = bf16[16,128,3,1024]{3,1,2,0:T(8,128)(2,1)} async-done(((bf16[16,128,3,1024]{3,1,2,0:T(8,128)(2,1)}), bf16[16,128,3,1024]{3,1,2,0:T(8,128)(2,1)}, u32[]{:S(2)}, u32[]{:S(2)}) %all-to-all-start) | async-done | bytes 12582944 | tf_op jit(solution)/shard_map/all_to_all | solution.py:103
  301.1 11.1 %gather_fusion = bf16[16,128,3,1024]{3,1,2,0:T(8,128)(2,1)} fusion(bf16[16,128,3,1024]{3,1,2,0:T(8,128)(2,1)} %all-to-all-done, s32[1024]{0:T(1024)S(1)} %pad_clamp_fusion.1), kind=kCustom, calls=%fused_computation.2 | custom fusion | bytes 25165888 | tf_op jit(solution)/shard_map/jit(_take)/gather | solution.py:107
  312.2 6.5 broadcast_select_fusion.1
  318.8 4.9 fusion.169
  323.6 6.4 copy.122
  330.0 6.4 copy.127
  336.4 6.5 copy.118
  342.9 9.9 fusion.172
  352.8 9.9 fusion.171
  362.7 10.4 fusion.60
  373.1 19.0 %fusion.14 = (f32[16]{0:T(128)S(1)}, f32[16]{0:T(128)S(1)}, f32[8,16,128,256]{3,2,1,0:T(8,128)}) fusion(f32[8,256]{1,0:T(8,128)S(1)} %copy-done.6, f32[8,16,128,256]{3,2,1,0:T(8,128)} %fusion.60, bf16[8,128,256]{2,1,0:T(8,128)(2,1)S(1)} %copy-done, bf16[16,128,8,128]{1,3,2,0:T(8,128)(2,1)} %bitcast.196, f32[16,8,128,128]{2,3,1,0:T(8,128)} %get-tuple-element.42, ...), kind=kOutput, calls=%fused_computation.26 | convolution fusion | flops 1667235840 | bytes 46735488 | tf_op jit(solution)/shard_map/plhd,hdr->plhr/dot_general | solution.py:25
  392.1 7.1 psum.14
  399.2 0.6 fusion.151
  399.9 9.9 convert_bitcast_fusion.1
  409.9 6.3 fusion.80
  416.2 9.7 fusion.110
  425.9 10.3 convert_bitcast_fusion
  436.2 2.0 copy-done.5
  438.2 6.3 fusion.76
  444.5 18.0 %fusion.101 = f32[16,128,1,8,128]{1,4,3,0,2:T(8,128)} fusion(bf16[16,128,8,128]{1,3,2,0:T(8,128)(2,1)} %bitcast.195, f32[16,8,128,128]{2,3,1,0:T(8,128)} %fusion.76, f32[16,8,128,128]{2,3,1,0:T(8,128)} %get-tuple-element.42, f32[16,8,128]{2,1,0:T(8,128)S(1)} %get-tuple-element.41), kind=kOutput, calls=%fused_computation.95 | convolution fusion | flops 551567488 | bytes 29425664 | tf_op jit(solution)/shard_map/phlm,pmhd->plhd/dot_general | solution.py:53
  462.5 18.1 %fusion.107 = f32[16,128,1,8,128]{1,4,3,0,2:T(8,128)} fusion(bf16[16,128,8,128]{1,3,2,0:T(8,128)(2,1)} %bitcast.193, f32[16,8,128,128]{2,3,1,0:T(8,128)} %fusion.80, f32[16,8,128,128]{2,3,1,0:T(8,128)} %get-tuple-element.44, f32[16,8,128]{2,1,0:T(8,128)S(1)} %get-tuple-element.43), kind=kOutput, calls=%fused_computation.97 | convolution fusion | flops 551567488 | bytes 29425664 | tf_op jit(solution)/shard_map/phlm,plhd->pmhd/dot_general | solution.py:54
  480.5 18.7 %pad_maximum_fusion.1 = f32[16,128,3,8,128]{1,4,3,0,2:T(8,128)} fusion(f32[16,128,1,8,128]{1,4,3,0,2:T(8,128)} %fusion.110, f32[16,128,1,8,128]{1,4,3,0,2:T(8,128)} %fusion.107, f32[16,128,1,8,128]{1,4,3,0,2:T(8,128)} %fusion.101), kind=kLoop, calls=%fused_computation.18 | loop fusion | flops 12582912 | bytes 50331648 | tf_op jit(solution)/shard_map/stack | solution.py:126
  499.2 24.7 %copy.147 = f32[16,128,3,8,128]{4,3,2,1,0:T(8,128)} copy(f32[16,128,3,8,128]{1,4,3,0,2:T(8,128)} %pad_maximum_fusion.1) | data formatting | bytes 50331648 | tf_op jit(solution)/shard_map/stack | solution.py:126
  523.9 34.5 %convolution_convert_fusion = bf16[16,393216]{1,0:T(8,128)(2,1)} fusion(f32[2,8,3072,128]{3,2,1,0:T(8,128)} %bitcast.189, s32[16]{0:T(128)S(1)} %copy-done.10), kind=kOutput, calls=%fused_computation.9 | convolution fusion | flops 1214251264 | bytes 37748800 | tf_op jit(solution)/shard_map/dot_general | solution.py:136
  558.4 30.0 %reshape.150 = bf16[16,128,3,1024]{3,2,1,0:T(4,128)(2,1)} reshape(bf16[16,393216]{1,0:T(8,128)(2,1)} %convolution_convert_fusion) | data formatting | bytes 25165824 | tf_op jit(solution)/shard_map/reshape | solution.py:139
  588.4 12.2 %copy.148 = bf16[16,128,3,1024]{3,1,2,0:T(8,128)(2,1)} copy(bf16[16,128,3,1024]{3,2,1,0:T(4,128)(2,1)} %reshape.150) | data formatting | bytes 25165824 | tf_op jit(solution)/shard_map/reshape | solution.py:139
  600.6 6.6 all-to-all-start.1
  607.2 0.7 slice_bitcast_fusion.2
  607.9 281.0 %psum.15 = f32[]{:T(128)} all-reduce(f32[]{:T(128)} %get-tuple-element.39), channel_id=1, replica_groups=mesh['group'=8,'fsdp'=4] {'group'}, use_global_device_ids=true, to_apply=%region_15.17 | all-reduce | flops 1 | bytes 8 | tf_op jit(solution)/shard_map/psum | solution.py:116
  888.9 18.1 %fusion.98 = f32[16,128,1,8,128]{1,4,3,0,2:T(8,128)} fusion(bf16[16,128,8,128]{1,3,2,0:T(8,128)(2,1)} %bitcast.199, f32[16,8,128,128]{2,3,1,0:T(8,128)} %fusion.76, f32[16,8,128,128]{2,3,1,0:T(8,128)} %get-tuple-element.42, f32[16,8,128]{2,1,0:T(8,128)S(1)} %get-tuple-element.41), kind=kOutput, calls=%fused_computation.94 | convolution fusion | flops 551567488 | bytes 29425664 | tf_op jit(solution)/shard_map/phlm,plhd->pmhd/dot_general | solution.py:54
  907.0 17.9 %fusion.104 = f32[16,128,1,8,128]{1,4,3,0,2:T(8,128)} fusion(bf16[16,128,8,128]{1,3,2,0:T(8,128)(2,1)} %bitcast.201, f32[16,8,128,128]{2,3,1,0:T(8,128)} %fusion.80, f32[16,8,128,128]{2,3,1,0:T(8,128)} %get-tuple-element.44, f32[16,8,128]{2,1,0:T(8,128)S(1)} %get-tuple-element.43), kind=kOutput, calls=%fused_computation.96 | convolution fusion | flops 551567488 | bytes 29425664 | tf_op jit(solution)/shard_map/phlm,pmhd->plhd/dot_general | solution.py:53
  924.9 11.1 %fusion.113 = f32[16,128,1,8,128]{1,4,3,0,2:T(8,128)} fusion(bf16[16,128,8,128]{3,1,0,2:T(8,128)(2,1)} %copy-done.5, f32[16,8,128,128]{2,3,1,0:T(8,128)} %get-tuple-element.42, f32[16,8,128]{2,1,0:T(8,128)S(1)} %get-tuple-element.41), kind=kOutput, calls=%fused_computation.99 | convolution fusion | flops 541065216 | bytes 21037056 | tf_op jit(solution)/shard_map/phlm,plhd->pmhd/dot_general | solution.py:42
  936.0 15.5 %pad_maximum_fusion = f32[16,128,3,8,128]{1,4,3,0,2:T(8,128)} fusion(f32[16,128,1,8,128]{1,4,3,0,2:T(8,128)} %fusion.113, f32[16,128,1,8,128]{1,4,3,0,2:T(8,128)S(1)} %copy-done.4, f32[16,128,1,8,128]{1,4,3,0,2:T(8,128)} %fusion.104), kind=kLoop, calls=%fused_computation.17 | loop fusion | flops 12582912 | bytes 50331648 | tf_op jit(solution)/shard_map/stack | solution.py:125
  951.5 24.8 %copy.142 = f32[16,128,3,8,128]{4,3,2,1,0:T(8,128)} copy(f32[16,128,3,8,128]{1,4,3,0,2:T(8,128)} %pad_maximum_fusion) | data formatting | bytes 50331648 | tf_op jit(solution)/shard_map/stack | solution.py:125
  976.9 31.1 %fusion.7 = f32[8,393216]{1,0:T(8,128)} fusion(f32[2,8,3072,128]{3,2,1,0:T(8,128)} %bitcast.190, s32[16]{0:T(128)S(1)} %slice_bitcast_fusion.2), kind=kOutput, calls=%fused_computation.14 | convolution fusion | flops 603979904 | bytes 37748800 | tf_op jit(solution)/shard_map/dot_general | solution.py:130
  1008.0 18.7 %copy.149 = bf16[16,128,3,1024]{3,2,1,0:T(4,128)(2,1)} copy(bf16[16,128,3,1024]{3,1,2,0:T(8,128)(2,1)} %all-to-all-done.1) | data formatting | bytes 25165824 | tf_op jit(solution)/shard_map/all_to_all | solution.py:140
  1026.7 28.8 %reshape.151 = bf16[16,393216]{1,0:T(8,128)(2,1)} reshape(bf16[16,128,3,1024]{3,2,1,0:T(4,128)(2,1)} %copy.149) | data formatting | bytes 25165824 | tf_op jit(solution)/shard_map/reshape | solution.py:146
  1055.5 10.0 fusion.4
  1065.6 6.2 copy.150
  (55 shorter events, 0.5 us)
Async XLA Ops:
  0.6 362.1 %copy-start = (bf16[8,128,256]{2,1,0:T(8,128)(2,1)S(1)}, bf16[8,128,256]{2,1,0:T(8,128)(2,1)}, u32[]{:S(2)}) copy-start(bf16[8,128,256]{2,1,0:T(8,128)(2,1)} %param.9) | copy-start | bytes 1572868
  1.8 11.6 %copy-start.9 = (s32[1,16,3]{1,2,0:T(4,128)}, s32[1,16,3]{1,2,0:T(4,128)S(1)}, u32[]{:S(2)}) copy-start(s32[1,16,3]{1,2,0:T(4,128)S(1)} %copy.226) | copy-start | bytes 580
  4.1 9.4 copy-start.11
  4.3 9.2 copy-start.7
  24.4 276.7 %all-to-all-start = ((bf16[16,128,3,1024]{3,1,2,0:T(8,128)(2,1)}), bf16[16,128,3,1024]{3,1,2,0:T(8,128)(2,1)}, u32[]{:S(2)}, u32[]{:S(2)}) async-start(bf16[16,128,3,1024]{3,1,2,0:T(8,128)(2,1)} %select_select_fusion), calls=%async_computation | async-start | bytes 25165824 | tf_op jit(solution)/shard_map/all_to_all | solution.py:103
  362.7 10.4 copy-start.6
  373.1 26.1 %copy-start.13 = (s32[16]{0:T(128)S(1)}, s32[16]{0:T(128)}, u32[]{:S(2)}) copy-start(s32[16]{0:T(128)} %param.11) | copy-start | bytes 196
  399.2 10.6 copy-start.14
  399.9 9.9 copy-start.3
  425.9 12.3 %copy-start.2 = (bf16[16,128,1,1024]{1,3,0,2:T(8,128)(2,1)S(1)}, bf16[16,128,1,1024]{1,3,0,2:T(8,128)(2,1)}, u32[]{:S(2)}) copy-start(bf16[16,128,1,1024]{1,3,0,2:T(8,128)(2,1)} %copy.126) | copy-start | bytes 12582916
  436.2 2.0 copy-start.5
  499.2 24.7 %copy-start.10 = (s32[16]{0:T(128)S(1)}, s32[16]{0:T(128)}, u32[]{:S(2)}) copy-start(s32[16]{0:T(128)} %get-tuple-element.26) | copy-start | bytes 196
  600.6 407.3 %all-to-all-start.1 = ((bf16[16,128,3,1024]{3,1,2,0:T(8,128)(2,1)}), bf16[16,128,3,1024]{3,1,2,0:T(8,128)(2,1)}, u32[]{:S(2)}, u32[]{:S(2)}) async-start(bf16[16,128,3,1024]{3,1,2,0:T(8,128)(2,1)} %copy.148), calls=%async_computation.1 | async-start | bytes 25165824 | tf_op jit(solution)/shard_map/all_to_all | solution.py:140
  924.9 11.1 %copy-start.4 = (f32[16,128,1,8,128]{1,4,3,0,2:T(8,128)S(1)}, f32[16,128,1,8,128]{1,4,3,0,2:T(8,128)}, u32[]{:S(2)}) copy-start(f32[16,128,1,8,128]{1,4,3,0,2:T(8,128)} %fusion.98) | copy-start | bytes 25165828
  1026.7 28.8 %copy-start.8 = (s32[16]{0:T(128)S(1)}, s32[16]{0:T(128)}, u32[]{:S(2)}) copy-start(s32[16]{0:T(128)} %copy-done.7) | copy-start | bytes 196
  1026.7 28.8 %copy-start.12 = (pred[16]{0:T(512)(128)(4,1)S(1)}, pred[16]{0:T(512)(128)(4,1)}, u32[]{:S(2)}) copy-start(pred[16]{0:T(512)(128)(4,1)} %copy-done.11) | copy-start | bytes 52
  1055.5 16.3 %copy-start.1 = (bf16[8,128,256]{2,1,0:T(8,128)(2,1)S(1)}, bf16[8,128,256]{2,1,0:T(8,128)(2,1)}, u32[]{:S(2)}) copy-start(bf16[8,128,256]{2,1,0:T(8,128)(2,1)} %param.9) | copy-start | bytes 1572868
where the time goes:
time: 1080 us; the launch traced here: 1070 us
  blocking collectives  288 us (27%)
  matrix products  250 us (23%)
  local copies, waits for them, and re-layouts  230 us (21%)
  waiting for transfers between devices  228 us (21%)
  other arithmetic  61.2 us (6%)
  starting transfers between devices  12.8 us (1%)
    psum x1, blocking collectives, local(): loss_sum = lax.psum(jnp.sum(loss_terms), 'group')  281 us
    all_to_all x1, waiting for transfers between devices, local(): lax.all_to_all(outgoing, 'group', split_axis=0, concat_axis=0, tiled=True)  228 us
    slice x8, local copies, waits for them, and re-layouts, split_heads(): rows_in[:, :, component]  48.1 us
    reshape x2, local copies, waits for them, and re-layouts, local(): outgoing_grad.astype(jnp.bfloat16).reshape(slots_all, length, 3, row_width)  42.3 us
    dot_general x2, matrix products, backward(): jnp.einsum('phlm,plhd->pmhd', dscores, query_rows, preferred_element_type...  36.2 us
    dot_general x2, matrix products, backward(): jnp.einsum('phlm,pmhd->plhd', dscores, key_rows, preferred_element_type=j...  35.9 us
    dot_general x1, matrix products, local(): jnp.dot(back_pick, grad_second, precision=lax.Precision.HIGHEST, preferre...  34.5 us
    dot_general x1, matrix products, local(): jnp.dot(own_pick, grad_first, precision=lax.Precision.HIGHEST, preferred_...  31.1 us
  transfers between devices with their start and end apart: 2, of which 1 were waited for; matrix products, arithmetic and copies ran while one was open for 15% of the time, Pallas kernels for 0%

commit v1 on v0

--- a/solution.py
+++ b/solution.py
@@ -4,6 +4,20 @@
 from jax.sharding import PartitionSpec as P
 
 loss_scale = 8192.0
+
+
+def update_spans_up(body, array_dim, here_x):
+    met_up = body.shape
+    field_out = body.reshape(
+        *met_up[:array_dim], here_x, met_up[array_dim] // here_x, *met_up[array_dim + 1 :]
+    )
+    return jnp.moveaxis(field_out, array_dim, 0)
+
+
+def _scan_islands(field, join_dim):
+    e_now = list(field.shape[1:])
+    e_now[join_dim] *= field.shape[0]
+    return jnp.moveaxis(field, 0, join_dim).reshape(e_now)
 
 
 def split_heads(rows_in, component, heads, head_dim):
@@ -100,7 +114,24 @@
     flat_valid = send_valid.reshape(slots_all)
     outgoing = jnp.take(mol_qkv, flat_member, axis=0)
     outgoing = jnp.where(flat_valid[:, None, None, None], outgoing, jnp.zeros_like(outgoing))
-    incoming = lax.all_to_all(outgoing, "group", split_axis=0, concat_axis=0, tiled=True)
+
+    def view_patches(target, ax_name, w_in, point):
+        part_next, v_next = (lax.axis_size(ax_name), lax.axis_index(ax_name))
+        p_next = update_spans_up(target, w_in, part_next)
+        all_rows = [p_next[v_next]]
+        for num in tuple(range(1, part_next)):
+            val = p_next[(v_next + num) % part_next]
+            all_rows.append(
+                lax.ppermute(
+                    val,
+                    axis_name=ax_name,
+                    perm=[(q, (q + num) % part_next) for q in range(part_next)],
+                )
+            )
+        p_next = jnp.stack(all_rows)[(v_next - jnp.arange(part_next)) % part_next]
+        return _scan_islands(p_next, point)
+
+    incoming = view_patches(outgoing, "group", 0, 0)
     my_pairs = lax.dynamic_index_in_dim(blocks, device, 0, keepdims=False)
     my_fetch = lax.dynamic_index_in_dim(fetch_slot, device, 0, keepdims=False)
     my_return = lax.dynamic_index_in_dim(return_slot, device, 0, keepdims=False)

time: 1080 us -> 1140 us (1.056)
  local copies, waits for them, and re-layouts: 230 us -> 263 us
  waiting for transfers between devices: 228 us -> 244 us
    ppermute x0 -> x7, waiting for transfers between devices: none -> 244 us  [view_patches(): lax.ppermute(val, axis_name=ax_name, perm=[(q, (q + num) % part_next) for...]
    all_to_all x1 -> x0, waiting for transfers between devices: 228 us -> none  [local(): lax.all_to_all(outgoing, 'group', split_axis=0, concat_axis=0, tiled=True)]
    unnamed x34 -> x42, local copies, waits for them, and re-layouts: 8.36 us -> 24 us
    dot_general x2, matrix products: 29.4 us -> 41.1 us  [forward(): jnp.einsum('plhd,hdr->plhr', context, head_proj, preferred_element_type=j...]
  transfers between devices with their start and end apart: 2 -> 8, of which waited for: 1 -> 3; matrix products, arithmetic and copies ran while one was open for 15% -> 16% of each run, Pallas kernels for 0% -> 0%
where the time goes in v1:
time: 1140 us; the launch traced here: 1130 us
  blocking collectives  286 us (25%)
  local copies, waits for them, and re-layouts  263 us (23%)
  matrix products  259 us (23%)
  waiting for transfers between devices  244 us (21%)
  other arithmetic  57.1 us (5%)
  starting transfers between devices  15.8 us (1%)
    psum x1, blocking collectives, local(): loss_sum = lax.psum(jnp.sum(loss_terms), 'group')  281 us
    ppermute x7, waiting for transfers between devices, view_patches(): lax.ppermute(val, axis_name=ax_name, perm=[(q, (q + num) % part_next) for...  244 us
    slice x8, local copies, waits for them, and re-layouts, split_heads(): rows_in[:, :, component]  48 us
    reshape x2, local copies, waits for them, and re-layouts, local(): outgoing_grad.astype(jnp.bfloat16).reshape(slots_all, length, 3, row_width)  42.1 us
    dot_general x2, matrix products, forward(): jnp.einsum('plhd,hdr->plhr', context, head_proj, preferred_element_type=j...  41.1 us
    dot_general x2, matrix products, backward(): jnp.einsum('phlm,plhd->pmhd', dscores, query_rows, preferred_element_type...  35.9 us
    dot_general x2, matrix products, backward(): jnp.einsum('phlm,pmhd->plhd', dscores, key_rows, preferred_element_type=j...  35.8 us
    dot_general x1, matrix products, local(): jnp.dot(back_pick, grad_second, precision=lax.Precision.HIGHEST, preferre...  34.7 us
  transfers between devices with their start and end apart: 8, of which 3 were waited for; matrix products, arithmetic and copies ran while one was open for 16% of the time, Pallas kernels for 0%

profile of v1, /device:TPU:8, one launch (start us, length us, event | category | flops | bytes accessed | tf_op | source)
XLA Modules:
  0.0 1127.0 jit_solution(12265406891173305766)
XLA Ops:
  0.8 0.8 reshape.199
  1.9 1.0 compare_reduce_fusion
  3.3 1.2 gather_fusion.2
  5.9 9.2 gather_fusion.4
  15.1 6.7 select_select_fusion
  21.8 4.7 dynamic-slice_bitcast_fusion
  26.5 3.5 collective-permute-start.4
  30.5 2.5 collective-permute-start.2
  33.0 1.4 collective-permute-start
  34.4 9.2 gather_fusion.5
  43.7 6.5 broadcast_select_fusion
  50.2 4.8 fusion.172
  55.1 1.0 gather_fusion.3
  56.3 210.0 %collective-permute-done.1 = bf16[2,128,3,1024]{3,1,2,0:T(8,128)(2,1)} collective-permute-done((bf16[2,128,3,1024]{3,1,2,0:T(8,128)(2,1)}, bf16[2,128,3,1024]{3,1,2,0:T(8,128)(2,1)}, u32[]{:S(2)}, u32[]{:S(2)}) %collective-permute-start.1) | collective-permute-done | bytes 1572896 | tf_op jit(solution)/shard_map/ppermute | solution.py:125
  266.8 6.4 copy.119
  273.2 6.4 copy.128
  279.6 6.4 copy.126
  286.0 2.8 bitcast_dynamic-update-slice_fusion.6
  288.7 2.8 bitcast_dynamic-update-slice_fusion.5
  291.5 2.8 bitcast_dynamic-update-slice_fusion.4
  294.3 2.8 bitcast_dynamic-update-slice_fusion.3
  297.0 1.3 bitcast_dynamic-update-slice_fusion.2
  298.4 5.8 collective-permute-done.5
  304.2 2.8 bitcast_dynamic-update-slice_fusion.1
  307.0 27.7 %collective-permute-done.6 = bf16[2,128,3,1024]{3,1,2,0:T(8,128)(2,1)S(1)} collective-permute-done((bf16[2,128,3,1024]{3,1,2,0:T(8,128)(2,1)}, bf16[2,128,3,1024]{3,1,2,0:T(8,128)(2,1)S(1)}, u32[]{:S(2)}, u32[]{:S(2)}) %collective-permute-start.6) | collective-permute-done | bytes 1572896 | tf_op jit(solution)/shard_map/ppermute | solution.py:125
  334.7 1.3 bitcast_dynamic-update-slice_fusion
  336.0 11.3 %gather_fusion = bf16[8,2,128,3,1024]{4,2,3,1,0:T(8,128)(2,1)} fusion(bf16[8,2,128,3,1024]{4,2,3,1,0:T(8,128)(2,1)} %bitcast_dynamic-update-slice_fusion, s32[1024]{0:T(1024)S(1)} %pad_clamp_fusion.2), kind=kCustom, calls=%fused_computation.2 | custom fusion | bytes 25165856 | tf_op jit(solution)/shard_map/gather | solution.py:131
  347.3 11.1 gather_fusion.1
  358.4 6.5 broadcast_select_fusion.1
  364.9 4.8 fusion.171
  369.7 6.4 copy.122
  376.1 6.4 copy.127
  382.5 6.4 copy.118
  388.9 10.0 fusion.173
  398.8 9.9 fusion.174
  408.7 10.4 fusion.60
  419.1 30.8 %fusion.14 = (f32[16]{0:T(128)S(1)}, f32[16]{0:T(128)S(1)}, f32[8,16,128,256]{3,2,1,0:T(8,128)}) fusion(f32[8,256]{1,0:T(8,128)S(1)} %copy-done.7, f32[8,16,128,256]{3,2,1,0:T(8,128)} %fusion.60, bf16[8,128,256]{2,1,0:T(8,128)(2,1)S(1)} %copy-done, bf16[16,128,8,128]{1,3,2,0:T(8,128)(2,1)} %bitcast.230, f32[16,8,128,128]{2,3,1,0:T(8,128)} %get-tuple-element.50, ...), kind=kOutput, calls=%fused_computation.27 | convolution fusion | flops 1667235840 | bytes 46735488 | tf_op jit(solution)/shard_map/plhd,hdr->plhr/dot_general | solution.py:39
  449.8 5.9 psum.14
  455.7 0.7 fusion.153
  456.5 9.9 convert_bitcast_fusion.1
  466.4 6.4 fusion.80
  472.8 6.3 fusion.110
  479.1 10.1 convert_bitcast_fusion
  489.2 1.9 copy-done.6
  491.1 6.4 fusion.76
  497.5 17.9 %fusion.101 = f32[16,128,1,8,128]{1,4,3,0,2:T(8,128)} fusion(bf16[16,128,8,128]{1,3,2,0:T(8,128)(2,1)} %bitcast.229, f32[16,8,128,128]{2,3,1,0:T(8,128)} %fusion.76, f32[16,8,128,128]{2,3,1,0:T(8,128)} %get-tuple-element.50, f32[16,8,128]{2,1,0:T(8,128)S(1)} %get-tuple-element.49), kind=kOutput, calls=%fused_computation.96 | convolution fusion | flops 551567488 | bytes 29425664 | tf_op jit(solution)/shard_map/phlm,pmhd->plhd/dot_general | solution.py:67
  515.4 17.9 %fusion.107 = f32[16,128,1,8,128]{1,4,3,0,2:T(8,128)} fusion(bf16[16,128,8,128]{1,3,2,0:T(8,128)(2,1)} %bitcast.227, f32[16,8,128,128]{2,3,1,0:T(8,128)} %fusion.80, f32[16,8,128,128]{2,3,1,0:T(8,128)} %get-tuple-element.52, f32[16,8,128]{2,1,0:T(8,128)S(1)} %get-tuple-element.51), kind=kOutput, calls=%fused_computation.98 | convolution fusion | flops 551567488 | bytes 29425664 | tf_op jit(solution)/shard_map/phlm,plhd->pmhd/dot_general | solution.py:68
  533.3 18.7 %pad_maximum_fusion.1 = f32[16,128,3,8,128]{1,4,3,0,2:T(8,128)} fusion(f32[16,128,1,8,128]{1,4,3,0,2:T(8,128)} %fusion.110, f32[16,128,1,8,128]{1,4,3,0,2:T(8,128)} %fusion.107, f32[16,128,1,8,128]{1,4,3,0,2:T(8,128)} %fusion.101), kind=kLoop, calls=%fused_computation.19 | loop fusion | flops 12582912 | bytes 50331648 | tf_op jit(solution)/shard_map/stack | solution.py:157
  552.0 24.7 %copy.147 = f32[16,128,3,8,128]{4,3,2,1,0:T(8,128)} copy(f32[16,128,3,8,128]{1,4,3,0,2:T(8,128)} %pad_maximum_fusion.1) | data formatting | bytes 50331648 | tf_op jit(solution)/shard_map/stack | solution.py:157
  576.7 34.7 %convolution_convert_fusion = bf16[16,393216]{1,0:T(8,128)(2,1)} fusion(f32[2,8,3072,128]{3,2,1,0:T(8,128)} %bitcast.221, s32[16]{0:T(128)S(1)} %copy-done.8), kind=kOutput, calls=%fused_computation.10 | convolution fusion | flops 1214251264 | bytes 37748800 | tf_op jit(solution)/shard_map/dot_general | solution.py:167
  611.4 29.9 %reshape.207 = bf16[16,128,3,1024]{3,2,1,0:T(4,128)(2,1)} reshape(bf16[16,393216]{1,0:T(8,128)(2,1)} %convolution_convert_fusion) | data formatting | bytes 25165824 | tf_op jit(solution)/shard_map/reshape | solution.py:170
  641.3 12.2 %copy.148 = bf16[16,128,3,1024]{3,1,2,0:T(8,128)(2,1)} copy(bf16[16,128,3,1024]{3,2,1,0:T(4,128)(2,1)} %reshape.207) | data formatting | bytes 25165824 | tf_op jit(solution)/shard_map/reshape | solution.py:170
  653.5 7.9 all-to-all-start
  662.1 280.5 %psum.15 = f32[]{:T(128)} all-reduce(f32[]{:T(128)} %get-tuple-element.47), channel_id=1, replica_groups=mesh['group'=8,'fsdp'=4] {'group'}, use_global_device_ids=true, to_apply=%region_15.17 | all-reduce | flops 1 | bytes 8 | tf_op jit(solution)/shard_map/psum | solution.py:147
  942.6 18.0 %fusion.98 = f32[16,128,1,8,128]{1,4,3,0,2:T(8,128)} fusion(bf16[16,128,8,128]{1,3,2,0:T(8,128)(2,1)} %bitcast.233, f32[16,8,128,128]{2,3,1,0:T(8,128)} %fusion.76, f32[16,8,128,128]{2,3,1,0:T(8,128)} %get-tuple-element.50, f32[16,8,128]{2,1,0:T(8,128)S(1)} %get-tuple-element.49), kind=kOutput, calls=%fused_computation.95 | convolution fusion | flops 551567488 | bytes 29425664 | tf_op jit(solution)/shard_map/phlm,plhd->pmhd/dot_general | solution.py:68
  960.6 17.9 %fusion.104 = f32[16,128,1,8,128]{1,4,3,0,2:T(8,128)} fusion(bf16[16,128,8,128]{1,3,2,0:T(8,128)(2,1)} %bitcast.235, f32[16,8,128,128]{2,3,1,0:T(8,128)} %fusion.80, f32[16,8,128,128]{2,3,1,0:T(8,128)} %get-tuple-element.52, f32[16,8,128]{2,1,0:T(8,128)S(1)} %get-tuple-element.51), kind=kOutput, calls=%fused_computation.97 | convolution fusion | flops 551567488 | bytes 29425664 | tf_op jit(solution)/shard_map/phlm,pmhd->plhd/dot_general | solution.py:67
  978.5 11.1 fusion.113
  989.5 15.5 %pad_maximum_fusion = f32[16,128,3,8,128]{1,4,3,0,2:T(8,128)} fusion(f32[16,128,1,8,128]{1,4,3,0,2:T(8,128)} %fusion.113, f32[16,128,1,8,128]{1,4,3,0,2:T(8,128)S(1)} %copy-done.5, f32[16,128,1,8,128]{1,4,3,0,2:T(8,128)} %fusion.104), kind=kLoop, calls=%fused_computation.18 | loop fusion | flops 12582912 | bytes 50331648 | tf_op jit(solution)/shard_map/stack | solution.py:156
  1005.0 24.7 %copy.142 = f32[16,128,3,8,128]{4,3,2,1,0:T(8,128)} copy(f32[16,128,3,8,128]{1,4,3,0,2:T(8,128)} %pad_maximum_fusion) | data formatting | bytes 50331648 | tf_op jit(solution)/shard_map/stack | solution.py:156
  1030.3 31.2 %fusion.7 = f32[8,393216]{1,0:T(8,128)} fusion(f32[2,8,3072,128]{3,2,1,0:T(8,128)} %bitcast.222, s32[16]{0:T(128)S(1)} %slice_bitcast_fusion.2), kind=kOutput, calls=%fused_computation.15 | convolution fusion | flops 603979904 | bytes 37748800 | tf_op jit(solution)/shard_map/dot_general | solution.py:161
  1061.6 18.7 %copy.149 = bf16[16,128,3,1024]{3,2,1,0:T(4,128)(2,1)} copy(bf16[16,128,3,1024]{3,1,2,0:T(8,128)(2,1)} %all-to-all-done) | data formatting | bytes 25165824 | tf_op jit(solution)/shard_map/all_to_all | solution.py:171
  1080.3 29.1 %reshape.208 = bf16[16,393216]{1,0:T(8,128)(2,1)} reshape(bf16[16,128,3,1024]{3,2,1,0:T(4,128)(2,1)} %copy.149) | data formatting | bytes 25165824 | tf_op jit(solution)/shard_map/reshape | solution.py:177
  1109.4 10.0 fusion.4
  1119.5 6.2 copy.150
  (80 shorter events, 4.1 us)
Async XLA Ops:
  0.6 408.1 %copy-start = (bf16[8,128,256]{2,1,0:T(8,128)(2,1)S(1)}, bf16[8,128,256]{2,1,0:T(8,128)(2,1)}, u32[]{:S(2)}) copy-start(bf16[8,128,256]{2,1,0:T(8,128)(2,1)} %param.9) | copy-start | bytes 1572868
  5.1 0.6 copy-start.12
  5.9 9.2 copy-start.10
  26.5 270.5 %collective-permute-start.4 = (bf16[2,128,3,1024]{3,1,2,0:T(8,128)(2,1)}, bf16[2,128,3,1024]{3,1,2,0:T(8,128)(2,1)S(1)}, u32[]{:S(2)}, u32[]{:S(2)}) collective-permute-start(bf16[2,128,3,1024]{3,1,2,0:T(8,128)(2,1)} %get-tuple-element.37), channel_id=1, source_target_pairs={{0,20},{4,24},{8,28},{12,0},{16,4},{20,8},{24,12},{28,16},{1,21},{... | collective-permute-start | bytes 4718600 | tf_op jit(solution)/shard_map/ppermute | solution.py:125
  30.0 264.3 %collective-permute-start.3 = (bf16[2,128,3,1024]{3,1,2,0:T(8,128)(2,1)}, bf16[2,128,3,1024]{3,1,2,0:T(8,128)(2,1)}, u32[]{:S(2)}, u32[]{:S(2)}) collective-permute-start(bf16[2,128,3,1024]{3,1,2,0:T(8,128)(2,1)} %get-tuple-element.38), channel_id=1, source_target_pairs={{0,16},{4,20},{8,24},{12,28},{16,0},{20,4},{24,8},{28,12},{1,17},{... | collective-permute-start | bytes 4718600 | tf_op jit(solution)/shard_map/ppermute | solution.py:125
  30.5 261.0 %collective-permute-start.2 = (bf16[2,128,3,1024]{3,1,2,0:T(8,128)(2,1)}, bf16[2,128,3,1024]{3,1,2,0:T(8,128)(2,1)}, u32[]{:S(2)}, u32[]{:S(2)}) collective-permute-start(bf16[2,128,3,1024]{3,1,2,0:T(8,128)(2,1)} %get-tuple-element.39), channel_id=1, source_target_pairs={{0,12},{4,16},{8,20},{12,24},{16,28},{20,0},{24,4},{28,8},{1,13},{... | collective-permute-start | bytes 4718600 | tf_op jit(solution)/shard_map/ppermute | solution.py:125
  33.0 233.2 %collective-permute-start.1 = (bf16[2,128,3,1024]{3,1,2,0:T(8,128)(2,1)}, bf16[2,128,3,1024]{3,1,2,0:T(8,128)(2,1)}, u32[]{:S(2)}, u32[]{:S(2)}) collective-permute-start(bf16[2,128,3,1024]{3,1,2,0:T(8,128)(2,1)} %get-tuple-element.40), channel_id=1, source_target_pairs={{0,8},{4,12},{8,16},{12,20},{16,24},{20,28},{24,0},{28,4},{1,9},{5... | collective-permute-start | bytes 4718600 | tf_op jit(solution)/shard_map/ppermute | solution.py:125
  33.0 252.9 %collective-permute-start = (bf16[2,128,3,1024]{3,1,2,0:T(8,128)(2,1)}, bf16[2,128,3,1024]{3,1,2,0:T(8,128)(2,1)}, u32[]{:S(2)}, u32[]{:S(2)}) collective-permute-start(bf16[2,128,3,1024]{3,1,2,0:T(8,128)(2,1)} %get-tuple-element.41), channel_id=1, source_target_pairs={{0,4},{4,8},{8,12},{12,16},{16,20},{20,24},{24,28},{28,0},{1,5},{5... | collective-permute-start | bytes 4718600 | tf_op jit(solution)/shard_map/ppermute | solution.py:125
  34.4 9.2 copy-start.9
  266.3 38.0 %collective-permute-start.5 = (bf16[2,128,3,1024]{3,1,2,0:T(8,128)(2,1)}, bf16[2,128,3,1024]{3,1,2,0:T(8,128)(2,1)}, u32[]{:S(2)}, u32[]{:S(2)}) collective-permute-start(bf16[2,128,3,1024]{3,1,2,0:T(8,128)(2,1)} %get-tuple-element.36), channel_id=1, source_target_pairs={{0,24},{4,28},{8,0},{12,4},{16,8},{20,12},{24,16},{28,20},{1,25},{... | collective-permute-start | bytes 4718600 | tf_op jit(solution)/shard_map/ppermute | solution.py:125
  286.0 48.8 %collective-permute-start.6 = (bf16[2,128,3,1024]{3,1,2,0:T(8,128)(2,1)}, bf16[2,128,3,1024]{3,1,2,0:T(8,128)(2,1)S(1)}, u32[]{:S(2)}, u32[]{:S(2)}) collective-permute-start(bf16[2,128,3,1024]{3,1,2,0:T(8,128)(2,1)} %get-tuple-element.35), channel_id=1, source_target_pairs={{0,28},{4,0},{8,4},{12,8},{16,12},{20,16},{24,20},{28,24},{1,29},{... | collective-permute-start | bytes 4718600 | tf_op jit(solution)/shard_map/ppermute | solution.py:125
  408.7 10.4 copy-start.7
  419.1 36.7 %copy-start.14 = (s32[16]{0:T(128)S(1)}, s32[16]{0:T(128)}, u32[]{:S(2)}) copy-start(s32[16]{0:T(128)} %param.11) | copy-start | bytes 196
  455.7 0.7 copy-start.15
  456.5 9.9 copy-start.3
  466.4 6.4 copy-start.4
  479.1 12.0 %copy-start.2 = (bf16[16,128,1,1024]{1,3,0,2:T(8,128)(2,1)S(1)}, bf16[16,128,1,1024]{1,3,0,2:T(8,128)(2,1)}, u32[]{:S(2)}) copy-start(bf16[16,128,1,1024]{1,3,0,2:T(8,128)(2,1)} %copy.126) | copy-start | bytes 12582916
  489.2 1.9 copy-start.6
  552.0 24.7 %copy-start.8 = (s32[16]{0:T(128)S(1)}, s32[16]{0:T(128)}, u32[]{:S(2)}) copy-start(s32[16]{0:T(128)} %get-tuple-element.26) | copy-start | bytes 196
  653.5 408.0 %all-to-all-start = ((bf16[16,128,3,1024]{3,1,2,0:T(8,128)(2,1)}), bf16[16,128,3,1024]{3,1,2,0:T(8,128)(2,1)}, u32[]{:S(2)}, u32[]{:S(2)}) async-start(bf16[16,128,3,1024]{3,1,2,0:T(8,128)(2,1)} %copy.148), calls=%async_computation | async-start | bytes 25165824 | tf_op jit(solution)/shard_map/all_to_all | solution.py:171
  978.5 11.1 copy-start.5
  1080.3 29.1 %copy-start.11 = (pred[16]{0:T(512)(128)(4,1)S(1)}, pred[16]{0:T(512)(128)(4,1)}, u32[]{:S(2)}) copy-start(pred[16]{0:T(512)(128)(4,1)} %copy-done.10) | copy-start | bytes 52
  1080.3 29.1 %copy-start.13 = (s32[16]{0:T(128)S(1)}, s32[16]{0:T(128)}, u32[]{:S(2)}) copy-start(s32[16]{0:T(128)} %copy-done.12) | copy-start | bytes 196
  1109.4 16.3 %copy-start.1 = (bf16[8,128,256]{2,1,0:T(8,128)(2,1)S(1)}, bf16[8,128,256]{2,1,0:T(8,128)(2,1)}, u32[]{:S(2)}) copy-start(bf16[8,128,256]{2,1,0:T(8,128)(2,1)} %param.9) | copy-start | bytes 1572868
